TPU v7x, 32 devices: a whole 2x2x4 slice. The times are simulated.
32 devices in a mesh: groups: 2 (over y), pix: 8 (over z, x), dp: 2 (over core).
Axes of the slice: x: 2, y: 2, z: 4, core: 2. Of those that a mesh axis runs over, the one named last changes fastest.
Arguments:
- features: bfloat16 [64, 64, 512], P('pix', None, ('groups', 'dp')), parts along dimension 2, may hold values from -6 to 6
- cheb_weights: bfloat16 [4, 64, 64], replicated, may hold values from -0.375 to 0.375
- out_bias: float32 [64], replicated, may hold values from -3 to 3
- lap_tiles: bfloat16 [64, 64, 576], P('pix'), as said below
- neighbours: int32 [64, 2], P('pix'), may hold values from 0 to 15, as said below
- send_blocks: int32 [8, 4, 2], P('pix'), may hold values from 0 to 7, as said below
- pixel_mask: int32 [64, 64], P('pix'), may hold values 0 or 1
- cotangent: bfloat16 [64, 64, 512], P('pix', None, ('groups', 'dp')), parts along dimension 2, may hold values from -6 to 6
Outputs:
- output_maps: bfloat16 [64, 64, 512], P('pix', None, ('groups', 'dp')), parts along dimension 2
- grad_features: bfloat16 [64, 64, 512], P('pix', None, ('groups', 'dp')), parts along dimension 2
- grad_weights: float32 [8, 64, 64], P('groups'), parts along dimension 0
- grad_bias: float32 [128], P('groups'), parts along dimension 0
There are 2 independent parts, one for each index of `groups`. A program takes and returns all parts, laid end to end along the dimension named above; an argument that names none is the same for every part. Nothing has to cross between parts.
Inputs may be any that keep to these rules, and one draw needn't show every extreme that they name: `send_blocks`: for device p and direction d (to devices p + 1, p - 1, p + 2, p - 2 modulo 8, in this order), 2 distinct local block numbers of device p; no block is listed in two directions. `neighbours`: column 0 names a local block or a received slot 8 + d * 2 + s; every received slot is named by exactly one row, every local block by column 0 of at most one row. Column 1 names a local block other than the row's own, every local block by exactly one row. Both neighbour relations are symmetric. `lap_tiles`: the operator is symmetric: the tile of block b in the row of block a is the transpose of the tile of block a in the row of block b, and a block's own tile is symmetric.
All inputs are finite; a program needn't handle non-finite values. No bound on the sum of `pixel_mask` on one device may be relied on, other than what follows from the above.
Results may differ from a plain program's by a relative error of at most 0.0047.
Values may be sent and summed in bfloat16 or wider, within the bound.
No kernel may reach another device: no remote copies, remote signals or barrier semaphores. Data moves between devices by JAX's collectives and lax.ppermute only.
A program may use at most 64 MiB of HBM per device.

v0:
```python
import math
import jax
import jax.numpy as jnp
from jax import lax
from jax.sharding import PartitionSpec as P

DIRECTIONS = (1, -1, 2, -2)
CYCLE_STEPS = (0, -1, 1, -2, 2, -3, 3)


def shifted(block, axis, distance):
    devices = range(lax.axis_size(axis))
    route = [((i - distance) % len(devices), i) for i in devices]
    return lax.ppermute(block, axis, route)


def collect_halo(masked_values, outgoing):
    pieces = []
    for heading_index, travel in enumerate(DIRECTIONS):
        pieces.append(shifted(masked_values[outgoing[heading_index]], "pix", travel))
    return jnp.concatenate(pieces, axis=0)


def tile_product(masked_values, extended, lap_tiles, neighbours, keep_mask):
    block_count, pixel_count, lane_count = masked_values.shape
    columns = [jnp.roll(masked_values, -offset, axis=0) for offset in CYCLE_STEPS]
    columns.append(extended[neighbours[:, 0]])
    columns.append(extended[neighbours[:, 1]])
    picked = jnp.stack(columns, axis=1).reshape(block_count, -1, lane_count)
    product = jnp.einsum("bpk,bkl->bpl", lap_tiles, picked, preferred_element_type=jnp.float32)
    return product * keep_mask


def forward_apply(values, lap_tiles, neighbours, outgoing, keep_mask):
    masked_values = values * keep_mask
    halo_blocks = collect_halo(masked_values, outgoing)
    extended = jnp.concatenate([masked_values, halo_blocks], axis=0)
    return tile_product(masked_values, extended, lap_tiles, neighbours, keep_mask)


def pushed_apply(values, lap_tiles, neighbours, outgoing, keep_mask):
    masked_values = values * keep_mask
    block_count, pixel_count, lane_count = values.shape
    cycle_count = len(CYCLE_STEPS)
    partial_terms = jnp.einsum(
        "bpk,bpl->bkl", lap_tiles, masked_values, preferred_element_type=jnp.float32
    )
    partial_terms = partial_terms.reshape(block_count, -1, pixel_count, lane_count)
    running = jnp.zeros((block_count, pixel_count, lane_count), jnp.float32)
    for column, offset in enumerate(CYCLE_STEPS):
        running = running + jnp.roll(partial_terms[:, column], offset, axis=0)
    slot_count = outgoing.shape[1]
    halo_count = len(DIRECTIONS) * slot_count
    irregular = jnp.concatenate(
        [partial_terms[:, cycle_count], partial_terms[:, cycle_count + 1]], axis=0
    )
    target_ids = jnp.concatenate([neighbours[:, 0], neighbours[:, 1]], axis=0)
    pooled = jax.ops.segment_sum(irregular, target_ids, num_segments=block_count + halo_count)
    running = running + pooled[:block_count]
    returned_all = pooled[block_count:].reshape(
        len(DIRECTIONS), slot_count, pixel_count, lane_count
    )
    for heading_index, travel in enumerate(DIRECTIONS):
        returned = shifted(returned_all[heading_index], "pix", -travel)
        running = running.at[outgoing[heading_index]].add(returned)
    return running * keep_mask


def local(
    features, cheb_weights, out_bias, lap_tiles, neighbours, send_blocks, pixel_mask, cotangent
):
    block_count, pixel_count, lane_count = features.shape
    term_count, chan_in, chan_out = cheb_weights.shape
    map_count = lane_count // chan_in
    outgoing = send_blocks[0]
    keep_mask = pixel_mask.astype(jnp.bfloat16)[:, :, None]
    cheb_terms = [features]
    for degree in range(1, term_count):
        applied = forward_apply(cheb_terms[-1], lap_tiles, neighbours, outgoing, keep_mask)
        if degree == 1:
            cheb_terms.append(applied.astype(jnp.bfloat16))
        else:
            cheb_terms.append((2.0 * applied - cheb_terms[-2]).astype(jnp.bfloat16))
    flat_rows = block_count * pixel_count
    mixed_sum = jnp.zeros((flat_rows, map_count, chan_out), jnp.float32)
    for degree in range(term_count):
        term_block = cheb_terms[degree].reshape(flat_rows, map_count, chan_in)
        mixed_sum = mixed_sum + jnp.einsum(
            "rmc,co->rmo", term_block, cheb_weights[degree], preferred_element_type=jnp.float32
        )
    output_maps = (
        (mixed_sum + out_bias)
        .reshape(block_count, pixel_count, map_count * chan_out)
        .astype(jnp.bfloat16)
    )
    upstream = cotangent.reshape(flat_rows, map_count, chan_out)

    def direct(degree):
        return jnp.einsum(
            "rmo,co->rmc", upstream, cheb_weights[degree], preferred_element_type=jnp.float32
        ).reshape(block_count, pixel_count, lane_count)

    def adjoint(values):
        return pushed_apply(values, lap_tiles, neighbours, outgoing, keep_mask)

    adjoints = [None] * term_count
    for degree in range(term_count - 1, 0, -1):
        running = direct(degree)
        if degree + 1 < term_count:
            running = running + 2.0 * adjoint(adjoints[degree + 1])
        if degree + 2 < term_count:
            running = running - adjoints[degree + 2]
        adjoints[degree] = running.astype(jnp.bfloat16)
    running = direct(0) + adjoint(adjoints[1]) - adjoints[2]
    grad_features = running.astype(jnp.bfloat16)
    grad_list = []
    for degree in range(term_count):
        term_block = cheb_terms[degree].reshape(flat_rows, map_count, chan_in)
        grad_list.append(
            jnp.einsum("rmc,rmo->co", term_block, upstream, preferred_element_type=jnp.float32)
        )
    partial_grads = jnp.stack(grad_list)
    bias_part = jnp.sum(upstream.astype(jnp.float32), axis=(0, 1))
    summed_weights, summed_bias = lax.psum((partial_grads, bias_part), ("pix", "dp"))
    factor = 1.0 / math.sqrt(flat_rows * map_count * lax.axis_size("pix") * lax.axis_size("dp"))
    return (output_maps, grad_features, summed_weights * factor, summed_bias * factor)


def solution(mesh):
    return jax.shard_map(
        local,
        mesh=mesh,
        in_specs=(
            P("pix", None, ("groups", "dp")),
            P(),
            P(),
            P("pix", None, None),
            P("pix", None),
            P("pix", None, None),
            P("pix", None),
            P("pix", None, ("groups", "dp")),
        ),
        out_specs=(
            P("pix", None, ("groups", "dp")),
            P("pix", None, ("groups", "dp")),
            P("groups", None, None),
            P("groups"),
        ),
        check_vma=False,
    )
```

profile of v0, /device:TPU:8, one launch (start us, length us, event | category | flops | bytes accessed | tf_op | source)
XLA Modules:
  0.0 317.3 jit_solution(6542873860701884093)
XLA Ops:
  9.0 1.7 constant_dynamic-update-slice_fusion.4
  11.9 1.5 collective-permute-start
  17.3 1.6 collective-permute-start.2
  26.8 3.0 scatter_fusion
  29.8 1.7 fusion.90
  31.5 2.2 collective-permute-start.12
  47.2 1.6 fusion.70
  48.8 1.5 convert_reduce_fusion
  52.8 24.3 %psum.15 = f32[64]{0:T(128)} all-reduce(f32[64]{0:T(128)} %reduce_sum.18), channel_id=1, replica_groups=mesh['groups'=2,'pix'=8,'dp'=2] {'pix','dp'}, use_global_device_ids=true, to_apply=%region_18.19 | all-reduce | flops 64 | bytes 512 | tf_op jit(solution)/shard_map/psum | solution.py:124
  78.4 1.6 fusion.33
  81.4 1.5 fusion.35
  82.9 1.4 fusion.36
  84.4 1.6 fusion.37
  85.9 1.5 fusion.38
  93.6 7.7 %collective-permute-start.14 = (f32[2,64,128]{2,1,0:T(8,128)}, f32[2,64,128]{2,1,0:T(8,128)}, u32[]{:S(2)}, u32[]{:S(2)}) collective-permute-start(f32[2,64,128]{2,1,0:T(8,128)} %get-tuple-element.75), channel_id=1, source_target_pairs={{4,0},{6,2},{8,4},{10,6},{12,8},{14,10},{0,12},{2,14},{5,1},{7,3},... | collective-permute-start | bytes 196616 | tf_op jit(solution)/shard_map/ppermute | solution.py:14
  112.7 1.7 convolution_add_fusion.2
  118.4 3.9 %collective-permute-start.5 = (bf16[2,64,128]{2,1,0:T(8,128)(2,1)S(1)}, bf16[2,64,128]{2,1,0:T(8,128)(2,1)S(1)}, u32[]{:S(2)}, u32[]{:S(2)}) collective-permute-start(bf16[2,64,128]{2,1,0:T(8,128)(2,1)S(1)} %gather_fusion.7), channel_id=1, source_target_pairs={{2,0},{4,2},{6,4},{8,6},{10,8},{12,10},{14,12},{0,14},{3,1},{5,3},... | collective-permute-start | bytes 98312 | tf_op jit(solution)/shard_map/ppermute | solution.py:14
  123.9 2.0 collective-permute-start.6
  125.9 3.7 %collective-permute-done.6 = bf16[2,64,128]{2,1,0:T(8,128)(2,1)S(1)} collective-permute-done((bf16[2,64,128]{2,1,0:T(8,128)(2,1)S(1)}, bf16[2,64,128]{2,1,0:T(8,128)(2,1)S(1)}, u32[]{:S(2)}, u32[]{:S(2)}) %collective-permute-start.6) | collective-permute-done | bytes 32800 | tf_op jit(solution)/shard_map/ppermute | solution.py:14
  129.6 3.9 %collective-permute-start.7 = (bf16[2,64,128]{2,1,0:T(8,128)(2,1)S(1)}, bf16[2,64,128]{2,1,0:T(8,128)(2,1)S(1)}, u32[]{:S(2)}, u32[]{:S(2)}) collective-permute-start(bf16[2,64,128]{2,1,0:T(8,128)(2,1)S(1)} %gather_fusion.9), channel_id=1, source_target_pairs={{4,0},{6,2},{8,4},{10,6},{12,8},{14,10},{0,12},{2,14},{5,1},{7,3},... | collective-permute-start | bytes 98312 | tf_op jit(solution)/shard_map/ppermute | solution.py:14
  133.6 1.6 collective-permute-done.7
  160.2 2.0 collective-permute-start.8
  162.1 1.8 collective-permute-start.9
  163.9 3.5 %collective-permute-start.11 = (bf16[2,64,128]{2,1,0:T(8,128)(2,1)}, bf16[2,64,128]{2,1,0:T(8,128)(2,1)}, u32[]{:S(2)}, u32[]{:S(2)}) collective-permute-start(bf16[2,64,128]{2,1,0:T(8,128)(2,1)} %gather_fusion.15), channel_id=1, source_target_pairs={{4,0},{6,2},{8,4},{10,6},{12,8},{14,10},{0,12},{2,14},{5,1},{7,3},... | collective-permute-start | bytes 98312 | tf_op jit(solution)/shard_map/ppermute | solution.py:14
  168.5 1.9 pad_maximum_fusion.1
  171.2 3.3 %scatter_fusion.5 = f32[16,64,128]{2,1,0:T(8,128)} fusion(f32[16,64,128]{2,1,0:T(8,128)} %broadcast.94.clone.1, s32[16]{0:T(128)} %copy-done.72, f32[16,64,128]{2,1,0:T(8,128)} %pad_maximum_fusion.1), kind=kCustom, calls=%fused_computation.23 | custom fusion | flops 131072 | bytes 1572928 | tf_op jit(solution)/shard_map/scatter-add | solution.py:58
  174.6 1.8 fusion.89
  176.4 2.3 collective-permute-start.16
  178.8 1.6 convolution_add_fusion.1
  180.4 1.6 fusion.45
  182.0 1.6 fusion.46
  183.5 1.5 fusion.47
  185.1 1.4 fusion.48
  190.2 3.5 %collective-permute-start.18 = (f32[2,64,128]{2,1,0:T(8,128)}, f32[2,64,128]{2,1,0:T(8,128)S(1)}, u32[]{:S(2)}, u32[]{:S(2)}) collective-permute-start(f32[2,64,128]{2,1,0:T(8,128)} %get-tuple-element.71), channel_id=1, source_target_pairs={{4,0},{6,2},{8,4},{10,6},{12,8},{14,10},{0,12},{2,14},{5,1},{7,3},... | collective-permute-start | bytes 196616 | tf_op jit(solution)/shard_map/ppermute | solution.py:14
  197.9 1.6 gather_fusion.16
  199.5 1.6 gather_fusion.17
  210.9 1.6 fusion.31
  217.9 2.2 scatter_fusion.10
  220.8 3.0 collective-permute-start.20
  223.7 3.8 %collective-permute-start.22 = (f32[2,64,128]{2,1,0:T(8,128)}, f32[2,64,128]{2,1,0:T(8,128)}, u32[]{:S(2)}, u32[]{:S(2)}) collective-permute-start(f32[2,64,128]{2,1,0:T(8,128)} %get-tuple-element.67), channel_id=1, source_target_pairs={{4,0},{6,2},{8,4},{10,6},{12,8},{14,10},{0,12},{2,14},{5,1},{7,3},... | collective-permute-start | bytes 196616 | tf_op jit(solution)/shard_map/ppermute | solution.py:14
  227.6 2.3 slice_add_fusion
  229.9 68.8 %all-reduce.2.cloned.1.call-done = f32[4,64,64]{2,1,0:T(8,128)} async-done(((f32[4,64,64]{2,1,0:T(8,128)}), f32[4,64,64]{2,1,0:T(8,128)}) %all-reduce.2.cloned.1.call-update) | async-done | bytes 65552 | tf_op jit(solution)/shard_map/psum | solution.py:124
  298.7 1.6 broadcast_multiply_fusion
  300.2 2.1 scatter_fusion.11
  302.3 2.1 scatter_fusion.12
  304.4 2.2 scatter_fusion.13
  306.6 2.1 scatter_fusion.14
  308.7 1.8 subtract_convert_fusion
  (342 shorter events, 106.2 us)
Async XLA Ops:
  7.2 17.1 %copy-start = (bf16[8,64,576]{2,1,0:T(8,128)(2,1)S(1)}, bf16[8,64,576]{2,1,0:T(8,128)(2,1)}, u32[]{:S(2)}) copy-start(bf16[8,64,576]{2,1,0:T(8,128)(2,1)} %param.11) | copy-start | bytes 1769476
  7.2 291.5 %all-reduce.2.cloned.1.call-start = ((), (), s32[]{:S(2)}) async-start(), calls=%async_computation | async-start | bytes 262144 | tf_op jit(solution)/shard_map/psum | solution.py:124
  11.9 80.9 %collective-permute-start = (bf16[2,64,128]{2,1,0:T(8,128)(2,1)}, bf16[2,64,128]{2,1,0:T(8,128)(2,1)}, u32[]{:S(2)}, u32[]{:S(2)}) collective-permute-start(bf16[2,64,128]{2,1,0:T(8,128)(2,1)} %gather_fusion), channel_id=1, source_target_pairs={{14,0},{0,2},{2,4},{4,6},{6,8},{8,10},{10,12},{12,14},{15,1},{1,3}... | collective-permute-start | bytes 98312 | tf_op jit(solution)/shard_map/ppermute | solution.py:14
  14.6 79.0 %collective-permute-start.1 = (bf16[2,64,128]{2,1,0:T(8,128)(2,1)}, bf16[2,64,128]{2,1,0:T(8,128)(2,1)}, u32[]{:S(2)}, u32[]{:S(2)}) collective-permute-start(bf16[2,64,128]{2,1,0:T(8,128)(2,1)} %gather_fusion.1), channel_id=1, source_target_pairs={{2,0},{4,2},{6,4},{8,6},{10,8},{12,10},{14,12},{0,14},{3,1},{5,3},... | collective-permute-start | bytes 98312 | tf_op jit(solution)/shard_map/ppermute | solution.py:14
  17.3 84.8 %collective-permute-start.2 = (bf16[2,64,128]{2,1,0:T(8,128)(2,1)}, bf16[2,64,128]{2,1,0:T(8,128)(2,1)}, u32[]{:S(2)}, u32[]{:S(2)}) collective-permute-start(bf16[2,64,128]{2,1,0:T(8,128)(2,1)} %gather_fusion.2), channel_id=1, source_target_pairs={{12,0},{14,2},{0,4},{2,6},{4,8},{6,10},{8,12},{10,14},{13,1},{15,3... | collective-permute-start | bytes 98312 | tf_op jit(solution)/shard_map/ppermute | solution.py:14
  20.0 82.9 %collective-permute-start.3 = (bf16[2,64,128]{2,1,0:T(8,128)(2,1)}, bf16[2,64,128]{2,1,0:T(8,128)(2,1)}, u32[]{:S(2)}, u32[]{:S(2)}) collective-permute-start(bf16[2,64,128]{2,1,0:T(8,128)(2,1)} %gather_fusion.3), channel_id=1, source_target_pairs={{4,0},{6,2},{8,4},{10,6},{12,8},{14,10},{0,12},{2,14},{5,1},{7,3},... | collective-permute-start | bytes 98312 | tf_op jit(solution)/shard_map/ppermute | solution.py:14
  31.5 116.9 %collective-permute-start.12 = (f32[2,64,128]{2,1,0:T(8,128)}, f32[2,64,128]{2,1,0:T(8,128)}, u32[]{:S(2)}, u32[]{:S(2)}) collective-permute-start(f32[2,64,128]{2,1,0:T(8,128)} %get-tuple-element.77), channel_id=1, source_target_pairs={{2,0},{4,2},{6,4},{8,6},{10,8},{12,10},{14,12},{0,14},{3,1},{5,3},... | collective-permute-start | bytes 196616 | tf_op jit(solution)/shard_map/ppermute | solution.py:14
  46.4 33.6 %copy-start.32 = (bf16[7,64,128]{2,1,0:T(8,128)(2,1)S(1)}, bf16[7,64,128]{2,1,0:T(8,128)(2,1)}, u32[]{:S(2)}) copy-start(bf16[7,64,128]{2,1,0:T(8,128)(2,1)} %get-tuple-element.110) | copy-start | bytes 344068
  46.4 36.6 %copy-start.37 = (bf16[6,64,128]{2,1,0:T(8,128)(2,1)S(1)}, bf16[6,64,128]{2,1,0:T(8,128)(2,1)}, u32[]{:S(2)}) copy-start(bf16[6,64,128]{2,1,0:T(8,128)(2,1)} %get-tuple-element.106) | copy-start | bytes 294916
  46.4 39.5 %copy-start.50 = (bf16[3,64,128]{2,1,0:T(8,128)(2,1)S(1)}, bf16[3,64,128]{2,1,0:T(8,128)(2,1)}, u32[]{:S(2)}) copy-start(bf16[3,64,128]{2,1,0:T(8,128)(2,1)} %get-tuple-element.104) | copy-start | bytes 147460
  48.8 38.7 %copy-start.35 = (f32[3,64,128]{2,1,0:T(8,128)S(1)}, f32[3,64,128]{2,1,0:T(8,128)}, u32[]{:S(2)}) copy-start(f32[3,64,128]{2,1,0:T(8,128)} %get-tuple-element.52) | copy-start | bytes 294916
  48.8 38.7 %copy-start.55 = (f32[1,64,128]{2,1,0:T(8,128)S(1)}, f32[1,64,128]{2,1,0:T(8,128)}, u32[]{:S(2)}) copy-start(f32[1,64,128]{2,1,0:T(8,128)} %get-tuple-element.60) | copy-start | bytes 98308
  91.8 13.3 %copy-start.3 = (bf16[8,9,64,128]{3,2,0,1:T(8,128)(2,1)S(1)}, bf16[8,9,64,128]{3,2,0,1:T(8,128)(2,1)}, u32[]{:S(2)}) copy-start(bf16[8,9,64,128]{3,2,0,1:T(8,128)(2,1)} %fusion.38) | copy-start | bytes 3538948
  92.9 57.0 %collective-permute-start.13 = (f32[2,64,128]{2,1,0:T(8,128)}, f32[2,64,128]{2,1,0:T(8,128)}, u32[]{:S(2)}, u32[]{:S(2)}) collective-permute-start(f32[2,64,128]{2,1,0:T(8,128)} %get-tuple-element.76), channel_id=1, source_target_pairs={{14,0},{0,2},{2,4},{4,6},{6,8},{8,10},{10,12},{12,14},{15,1},{1,3}... | collective-permute-start | bytes 196616 | tf_op jit(solution)/shard_map/ppermute | solution.py:14
  93.6 57.7 %collective-permute-start.14 = (f32[2,64,128]{2,1,0:T(8,128)}, f32[2,64,128]{2,1,0:T(8,128)}, u32[]{:S(2)}, u32[]{:S(2)}) collective-permute-start(f32[2,64,128]{2,1,0:T(8,128)} %get-tuple-element.75), channel_id=1, source_target_pairs={{4,0},{6,2},{8,4},{10,6},{12,8},{14,10},{0,12},{2,14},{5,1},{7,3},... | collective-permute-start | bytes 196616 | tf_op jit(solution)/shard_map/ppermute | solution.py:14
  102.1 50.7 %collective-permute-start.15 = (f32[2,64,128]{2,1,0:T(8,128)}, f32[2,64,128]{2,1,0:T(8,128)}, u32[]{:S(2)}, u32[]{:S(2)}) collective-permute-start(f32[2,64,128]{2,1,0:T(8,128)} %get-tuple-element.74), channel_id=1, source_target_pairs={{12,0},{14,2},{0,4},{2,6},{4,8},{6,10},{8,12},{10,14},{13,1},{15,3... | collective-permute-start | bytes 196616 | tf_op jit(solution)/shard_map/ppermute | solution.py:14
  111.5 6.9 %collective-permute-start.4 = (bf16[2,64,128]{2,1,0:T(8,128)(2,1)}, bf16[2,64,128]{2,1,0:T(8,128)(2,1)}, u32[]{:S(2)}, u32[]{:S(2)}) collective-permute-start(bf16[2,64,128]{2,1,0:T(8,128)(2,1)} %gather_fusion.6), channel_id=1, source_target_pairs={{14,0},{0,2},{2,4},{4,6},{6,8},{8,10},{10,12},{12,14},{15,1},{1,3}... | collective-permute-start | bytes 98312 | tf_op jit(solution)/shard_map/ppermute | solution.py:14
  118.4 5.5 %collective-permute-start.5 = (bf16[2,64,128]{2,1,0:T(8,128)(2,1)S(1)}, bf16[2,64,128]{2,1,0:T(8,128)(2,1)S(1)}, u32[]{:S(2)}, u32[]{:S(2)}) collective-permute-start(bf16[2,64,128]{2,1,0:T(8,128)(2,1)S(1)} %gather_fusion.7), channel_id=1, source_target_pairs={{2,0},{4,2},{6,4},{8,6},{10,8},{12,10},{14,12},{0,14},{3,1},{5,3},... | collective-permute-start | bytes 98312 | tf_op jit(solution)/shard_map/ppermute | solution.py:14
  123.9 5.7 %collective-permute-start.6 = (bf16[2,64,128]{2,1,0:T(8,128)(2,1)S(1)}, bf16[2,64,128]{2,1,0:T(8,128)(2,1)S(1)}, u32[]{:S(2)}, u32[]{:S(2)}) collective-permute-start(bf16[2,64,128]{2,1,0:T(8,128)(2,1)S(1)} %gather_fusion.8), channel_id=1, source_target_pairs={{12,0},{14,2},{0,4},{2,6},{4,8},{6,10},{8,12},{10,14},{13,1},{15,3... | collective-permute-start | bytes 98312 | tf_op jit(solution)/shard_map/ppermute | solution.py:14
  129.6 5.5 %collective-permute-start.7 = (bf16[2,64,128]{2,1,0:T(8,128)(2,1)S(1)}, bf16[2,64,128]{2,1,0:T(8,128)(2,1)S(1)}, u32[]{:S(2)}, u32[]{:S(2)}) collective-permute-start(bf16[2,64,128]{2,1,0:T(8,128)(2,1)S(1)} %gather_fusion.9), channel_id=1, source_target_pairs={{4,0},{6,2},{8,4},{10,6},{12,8},{14,10},{0,12},{2,14},{5,1},{7,3},... | collective-permute-start | bytes 98312 | tf_op jit(solution)/shard_map/ppermute | solution.py:14
  139.3 13.5 %copy-start.62 = (s32[2]{0:T(128)S(1)}, s32[2]{0:T(128)}, u32[]{:S(2)}) copy-start(s32[2]{0:T(128)} %copy-done.61) | copy-start | bytes 28
  160.2 28.7 %collective-permute-start.8 = (bf16[2,64,128]{2,1,0:T(8,128)(2,1)}, bf16[2,64,128]{2,1,0:T(8,128)(2,1)}, u32[]{:S(2)}, u32[]{:S(2)}) collective-permute-start(bf16[2,64,128]{2,1,0:T(8,128)(2,1)} %gather_fusion.12), channel_id=1, source_target_pairs={{14,0},{0,2},{2,4},{4,6},{6,8},{8,10},{10,12},{12,14},{15,1},{1,3}... | collective-permute-start | bytes 98312 | tf_op jit(solution)/shard_map/ppermute | solution.py:14
  162.1 28.1 %collective-permute-start.9 = (bf16[2,64,128]{2,1,0:T(8,128)(2,1)}, bf16[2,64,128]{2,1,0:T(8,128)(2,1)}, u32[]{:S(2)}, u32[]{:S(2)}) collective-permute-start(bf16[2,64,128]{2,1,0:T(8,128)(2,1)} %gather_fusion.13), channel_id=1, source_target_pairs={{2,0},{4,2},{6,4},{8,6},{10,8},{12,10},{14,12},{0,14},{3,1},{5,3},... | collective-permute-start | bytes 98312 | tf_op jit(solution)/shard_map/ppermute | solution.py:14
  163.9 31.2 %collective-permute-start.10 = (bf16[2,64,128]{2,1,0:T(8,128)(2,1)}, bf16[2,64,128]{2,1,0:T(8,128)(2,1)}, u32[]{:S(2)}, u32[]{:S(2)}) collective-permute-start(bf16[2,64,128]{2,1,0:T(8,128)(2,1)} %gather_fusion.14), channel_id=1, source_target_pairs={{12,0},{14,2},{0,4},{2,6},{4,8},{6,10},{8,12},{10,14},{13,1},{15,3... | collective-permute-start | bytes 98312 | tf_op jit(solution)/shard_map/ppermute | solution.py:14
  163.9 32.6 %collective-permute-start.11 = (bf16[2,64,128]{2,1,0:T(8,128)(2,1)}, bf16[2,64,128]{2,1,0:T(8,128)(2,1)}, u32[]{:S(2)}, u32[]{:S(2)}) collective-permute-start(bf16[2,64,128]{2,1,0:T(8,128)(2,1)} %gather_fusion.15), channel_id=1, source_target_pairs={{4,0},{6,2},{8,4},{10,6},{12,8},{14,10},{0,12},{2,14},{5,1},{7,3},... | collective-permute-start | bytes 98312 | tf_op jit(solution)/shard_map/ppermute | solution.py:14
  174.5 12.7 %copy-start.2 = (f32[16,64,128]{2,1,0:T(8,128)S(1)}, f32[16,64,128]{2,1,0:T(8,128)}, u32[]{:S(2)}) copy-start(f32[16,64,128]{2,1,0:T(8,128)} %scatter_fusion.5) | copy-start | bytes 1572868
  174.5 12.7 %copy-start.18 = (f32[7,64,128]{2,1,0:T(8,128)S(1)}, f32[7,64,128]{2,1,0:T(8,128)}, u32[]{:S(2)}) copy-start(f32[7,64,128]{2,1,0:T(8,128)} %get-tuple-element.48) | copy-start | bytes 688132
  174.5 12.7 %copy-start.19 = (f32[7,64,128]{2,1,0:T(8,128)S(1)}, f32[7,64,128]{2,1,0:T(8,128)}, u32[]{:S(2)}) copy-start(f32[7,64,128]{2,1,0:T(8,128)} %get-tuple-element.49) | copy-start | bytes 688132
  174.5 12.7 %copy-start.22 = (f32[6,64,128]{2,1,0:T(8,128)S(1)}, f32[6,64,128]{2,1,0:T(8,128)}, u32[]{:S(2)}) copy-start(f32[6,64,128]{2,1,0:T(8,128)} %get-tuple-element.44) | copy-start | bytes 589828
  174.6 12.7 %copy-start.23 = (f32[6,64,128]{2,1,0:T(8,128)S(1)}, f32[6,64,128]{2,1,0:T(8,128)}, u32[]{:S(2)}) copy-start(f32[6,64,128]{2,1,0:T(8,128)} %get-tuple-element.45) | copy-start | bytes 589828
  174.6 12.7 %copy-start.26 = (f32[5,64,128]{2,1,0:T(8,128)S(1)}, f32[5,64,128]{2,1,0:T(8,128)}, u32[]{:S(2)}) copy-start(f32[5,64,128]{2,1,0:T(8,128)} %get-tuple-element.40) | copy-start | bytes 491524
  174.6 12.7 %copy-start.27 = (f32[5,64,128]{2,1,0:T(8,128)S(1)}, f32[5,64,128]{2,1,0:T(8,128)}, u32[]{:S(2)}) copy-start(f32[5,64,128]{2,1,0:T(8,128)} %get-tuple-element.41) | copy-start | bytes 491524
  174.6 12.7 %copy-start.33 = (f32[3,64,128]{2,1,0:T(8,128)S(1)}, f32[3,64,128]{2,1,0:T(8,128)}, u32[]{:S(2)}) copy-start(f32[3,64,128]{2,1,0:T(8,128)} %get-tuple-element.38) | copy-start | bytes 294916
  174.6 12.7 %copy-start.34 = (f32[3,64,128]{2,1,0:T(8,128)S(1)}, f32[3,64,128]{2,1,0:T(8,128)}, u32[]{:S(2)}) copy-start(f32[3,64,128]{2,1,0:T(8,128)} %get-tuple-element.39) | copy-start | bytes 294916
  174.6 12.7 %copy-start.44 = (f32[2,64,128]{2,1,0:T(8,128)S(1)}, f32[2,64,128]{2,1,0:T(8,128)}, u32[]{:S(2)}) copy-start(f32[2,64,128]{2,1,0:T(8,128)} %get-tuple-element.42) | copy-start | bytes 196612
  174.6 12.7 %copy-start.45 = (f32[2,64,128]{2,1,0:T(8,128)S(1)}, f32[2,64,128]{2,1,0:T(8,128)}, u32[]{:S(2)}) copy-start(f32[2,64,128]{2,1,0:T(8,128)} %get-tuple-element.43) | copy-start | bytes 196612
  174.6 12.7 %copy-start.53 = (f32[1,64,128]{2,1,0:T(8,128)S(1)}, f32[1,64,128]{2,1,0:T(8,128)}, u32[]{:S(2)}) copy-start(f32[1,64,128]{2,1,0:T(8,128)} %get-tuple-element.46) | copy-start | bytes 98308
  174.6 12.7 %copy-start.54 = (f32[1,64,128]{2,1,0:T(8,128)S(1)}, f32[1,64,128]{2,1,0:T(8,128)}, u32[]{:S(2)}) copy-start(f32[1,64,128]{2,1,0:T(8,128)} %get-tuple-element.47) | copy-start | bytes 98308
  176.4 31.1 %collective-permute-start.16 = (f32[2,64,128]{2,1,0:T(8,128)}, f32[2,64,128]{2,1,0:T(8,128)}, u32[]{:S(2)}, u32[]{:S(2)}) collective-permute-start(f32[2,64,128]{2,1,0:T(8,128)} %get-tuple-element.73), channel_id=1, source_target_pairs={{2,0},{4,2},{6,4},{8,6},{10,8},{12,10},{14,12},{0,14},{3,1},{5,3},... | collective-permute-start | bytes 196616 | tf_op jit(solution)/shard_map/ppermute | solution.py:14
  188.9 20.1 %collective-permute-start.17 = (f32[2,64,128]{2,1,0:T(8,128)}, f32[2,64,128]{2,1,0:T(8,128)S(1)}, u32[]{:S(2)}, u32[]{:S(2)}) collective-permute-start(f32[2,64,128]{2,1,0:T(8,128)} %get-tuple-element.72), channel_id=1, source_target_pairs={{14,0},{0,2},{2,4},{4,6},{6,8},{8,10},{10,12},{12,14},{15,1},{1,3}... | collective-permute-start | bytes 196616 | tf_op jit(solution)/shard_map/ppermute | solution.py:14
  190.2 19.4 %collective-permute-start.18 = (f32[2,64,128]{2,1,0:T(8,128)}, f32[2,64,128]{2,1,0:T(8,128)S(1)}, u32[]{:S(2)}, u32[]{:S(2)}) collective-permute-start(f32[2,64,128]{2,1,0:T(8,128)} %get-tuple-element.71), channel_id=1, source_target_pairs={{4,0},{6,2},{8,4},{10,6},{12,8},{14,10},{0,12},{2,14},{5,1},{7,3},... | collective-permute-start | bytes 196616 | tf_op jit(solution)/shard_map/ppermute | solution.py:14
  195.1 15.2 %collective-permute-start.19 = (f32[2,64,128]{2,1,0:T(8,128)}, f32[2,64,128]{2,1,0:T(8,128)S(1)}, u32[]{:S(2)}, u32[]{:S(2)}) collective-permute-start(f32[2,64,128]{2,1,0:T(8,128)} %get-tuple-element.70), channel_id=1, source_target_pairs={{12,0},{14,2},{0,4},{2,6},{4,8},{6,10},{8,12},{10,14},{13,1},{15,3... | collective-permute-start | bytes 196616 | tf_op jit(solution)/shard_map/ppermute | solution.py:14
  220.8 79.5 %collective-permute-start.20 = (f32[2,64,128]{2,1,0:T(8,128)}, f32[2,64,128]{2,1,0:T(8,128)}, u32[]{:S(2)}, u32[]{:S(2)}) collective-permute-start(f32[2,64,128]{2,1,0:T(8,128)} %get-tuple-element.69), channel_id=1, source_target_pairs={{2,0},{4,2},{6,4},{8,6},{10,8},{12,10},{14,12},{0,14},{3,1},{5,3},... | collective-permute-start | bytes 196616 | tf_op jit(solution)/shard_map/ppermute | solution.py:14
  223.7 78.6 %collective-permute-start.21 = (f32[2,64,128]{2,1,0:T(8,128)}, f32[2,64,128]{2,1,0:T(8,128)}, u32[]{:S(2)}, u32[]{:S(2)}) collective-permute-start(f32[2,64,128]{2,1,0:T(8,128)} %get-tuple-element.68), channel_id=1, source_target_pairs={{14,0},{0,2},{2,4},{4,6},{6,8},{8,10},{10,12},{12,14},{15,1},{1,3}... | collective-permute-start | bytes 196616 | tf_op jit(solution)/shard_map/ppermute | solution.py:14
  223.7 80.6 %collective-permute-start.22 = (f32[2,64,128]{2,1,0:T(8,128)}, f32[2,64,128]{2,1,0:T(8,128)}, u32[]{:S(2)}, u32[]{:S(2)}) collective-permute-start(f32[2,64,128]{2,1,0:T(8,128)} %get-tuple-element.67), channel_id=1, source_target_pairs={{4,0},{6,2},{8,4},{10,6},{12,8},{14,10},{0,12},{2,14},{5,1},{7,3},... | collective-permute-start | bytes 196616 | tf_op jit(solution)/shard_map/ppermute | solution.py:14
  227.6 79.0 %collective-permute-start.23 = (f32[2,64,128]{2,1,0:T(8,128)}, f32[2,64,128]{2,1,0:T(8,128)}, u32[]{:S(2)}, u32[]{:S(2)}) collective-permute-start(f32[2,64,128]{2,1,0:T(8,128)} %get-tuple-element.66), channel_id=1, source_target_pairs={{12,0},{14,2},{0,4},{2,6},{4,8},{6,10},{8,12},{10,14},{13,1},{15,3... | collective-permute-start | bytes 196616 | tf_op jit(solution)/shard_map/ppermute | solution.py:14
  227.6 79.0 %copy-start.64 = (s32[2]{0:T(128)S(1)}, s32[2]{0:T(128)}, u32[]{:S(2)}) copy-start(s32[2]{0:T(128)} %copy-done.61) | copy-start | bytes 28
  229.9 78.8 %copy-start.11 = (f32[8,64,128]{2,1,0:T(8,128)S(1)}, f32[8,64,128]{2,1,0:T(8,128)}, u32[]{:S(2)}) copy-start(f32[8,64,128]{2,1,0:T(8,128)} %copy.107) | copy-start | bytes 786436
  (54 other events, 274.6 us)
Sparse Core Ops, SparseCore 0:
  205.7 92.9 all-reduce.1
where the time goes:
time: 320 us; the launch traced here: 317 us
  local copies, waits for them, and re-layouts  76.6 us (24%)
  waiting for transfers between devices  75.9 us (24%)
  other arithmetic  63.2 us (20%)
  starting transfers between devices  44.7 us (14%)
  blocking collectives  24.3 us (8%)
  matrix products  17.3 us (5%)
  between operations  15.4 us (5%)
    psum x1, waiting for transfers between devices, local(): lax.psum((partial_grads, bias_part), ('pix', 'dp'))  68.8 us
    ppermute x24, starting transfers between devices, shifted(): return lax.ppermute(block, axis, route)  44.6 us
    psum x1, blocking collectives, local(): lax.psum((partial_grads, bias_part), ('pix', 'dp'))  24.3 us
    unnamed x19, other arithmetic  19.2 us
    scatter-add x12, other arithmetic, pushed_apply(): running = running.at[outgoing[heading_index]].add(returned)  17.4 us
    gather x12, local copies, waits for them, and re-layouts, collect_halo(): masked_values[outgoing[heading_index]]  13.1 us
    slice x18, local copies, waits for them, and re-layouts, pushed_apply(): running = running + jnp.roll(partial_terms[:, column], offset, axis=0)  13 us
    unnamed x170, local copies, waits for them, and re-layouts  12 us
  transfers between devices with their start and end apart: 25, of which 5 were waited for; matrix products, arithmetic and copies ran while one was open for 44% of the time, Pallas kernels for 0%

commit v1 on v0

--- a/solution.py
+++ b/solution.py
@@ -121,7 +121,7 @@
         )
     partial_grads = jnp.stack(grad_list)
     bias_part = jnp.sum(upstream.astype(jnp.float32), axis=(0, 1))
-    summed_weights, summed_bias = lax.psum((partial_grads, bias_part), ("pix", "dp"))
+    summed_weights, summed_bias = lax.psum(lax.psum((partial_grads, bias_part), "dp"), "pix")
     factor = 1.0 / math.sqrt(flat_rows * map_count * lax.axis_size("pix") * lax.axis_size("dp"))
     return (output_maps, grad_features, summed_weights * factor, summed_bias * factor)
 

time: 320 us -> 310 us (0.969)
  waiting for transfers between devices: 75.9 us -> 70.8 us
  starting transfers between devices: 44.7 us -> 40.5 us
    psum x1 -> x2, waiting for transfers between devices: 68.8 us -> 63.9 us  [the longest x1 63.9 us: local(): lax.psum(lax.psum((partial_grads, bias_part), 'dp'), 'pix')]
    ppermute x24, starting transfers between devices: 44.6 us -> 40.4 us  [shifted(): return lax.ppermute(block, axis, route)]
    psum x1 -> x2, blocking collectives: 24.3 us -> 21.2 us  [the longest x1 18.1 us: local(): lax.psum(lax.psum((partial_grads, bias_part), 'dp'), 'pix')]
    unnamed x170 -> x168, local copies, waits for them, and re-layouts: 12 us -> 12 us
  transfers between devices with their start and end apart: 25 -> 26, of which waited for: 5 -> 5; matrix products, arithmetic and copies ran while one was open for 44% -> 46% of each run, Pallas kernels for 0% -> 0%
where the time goes in v1:
time: 310 us; the launch traced here: 305 us
  local copies, waits for them, and re-layouts  76.7 us (25%)
  waiting for transfers between devices  70.8 us (23%)
  other arithmetic  63.3 us (20%)
  starting transfers between devices  40.5 us (13%)
  blocking collectives  21.2 us (7%)
  matrix products  17.3 us (6%)
  between operations  15.4 us (5%)
    psum x1, waiting for transfers between devices, local(): lax.psum(lax.psum((partial_grads, bias_part), 'dp'), 'pix')  63.9 us
    ppermute x24, starting transfers between devices, shifted(): return lax.ppermute(block, axis, route)  40.4 us
    unnamed x19, other arithmetic  19.2 us
    psum x1, blocking collectives, local(): lax.psum(lax.psum((partial_grads, bias_part), 'dp'), 'pix')  18.1 us
    scatter-add x12, other arithmetic, pushed_apply(): running = running.at[outgoing[heading_index]].add(returned)  17.4 us
    slice x18, local copies, waits for them, and re-layouts, pushed_apply(): running = running + jnp.roll(partial_terms[:, column], offset, axis=0)  13.1 us
    gather x12, local copies, waits for them, and re-layouts, collect_halo(): masked_values[outgoing[heading_index]]  13 us
    unnamed x168, local copies, waits for them, and re-layouts  12 us
  transfers between devices with their start and end apart: 26, of which 5 were waited for; matrix products, arithmetic and copies ran while one was open for 46% of the time, Pallas kernels for 0%

profile of v1, /device:TPU:8, one launch (start us, length us, event | category | flops | bytes accessed | tf_op | source)
XLA Modules:
  0.0 305.1 jit_solution(8863353574309804598)
XLA Ops:
  9.0 1.7 constant_dynamic-update-slice_fusion.4
  11.9 1.5 collective-permute-start
  14.6 1.4 collective-permute-start.1
  17.2 1.6 collective-permute-start.2
  26.8 3.0 scatter_fusion
  29.8 1.7 fusion.90
  31.6 2.2 collective-permute-start.12
  47.3 1.6 fusion.70
  48.9 1.5 convert_reduce_fusion
  53.0 3.1 %psum.30 = f32[64]{0:T(128)} all-reduce(f32[64]{0:T(128)} %reduce_sum.18), channel_id=1, replica_groups=mesh['groups'=2,'pix'=8,'dp'=2] {'dp'}, use_global_device_ids=true, to_apply=%region_19.20 | all-reduce | flops 64 | bytes 512 | tf_op jit(solution)/shard_map/psum | solution.py:124
  56.0 18.1 %psum.31 = f32[64]{0:T(128)} all-reduce(f32[64]{0:T(128)} %psum.30), channel_id=1, replica_groups=mesh['groups'=2,'pix'=8,'dp'=2] {'pix'}, use_global_device_ids=true, to_apply=%region_20.21 | all-reduce | flops 64 | bytes 512 | tf_op jit(solution)/shard_map/psum | solution.py:124
  75.4 1.5 fusion.33
  78.4 1.6 fusion.35
  81.3 1.5 fusion.37
  82.9 1.6 fusion.38
  90.8 3.3 %collective-permute-start.14 = (f32[2,64,128]{2,1,0:T(8,128)}, f32[2,64,128]{2,1,0:T(8,128)}, u32[]{:S(2)}, u32[]{:S(2)}) collective-permute-start(f32[2,64,128]{2,1,0:T(8,128)} %get-tuple-element.75), channel_id=1, source_target_pairs={{4,0},{6,2},{8,4},{10,6},{12,8},{14,10},{0,12},{2,14},{5,1},{7,3},... | collective-permute-start | bytes 196616 | tf_op jit(solution)/shard_map/ppermute | solution.py:14
  105.5 1.7 convolution_add_fusion.2
  111.0 3.9 %collective-permute-start.5 = (bf16[2,64,128]{2,1,0:T(8,128)(2,1)S(1)}, bf16[2,64,128]{2,1,0:T(8,128)(2,1)S(1)}, u32[]{:S(2)}, u32[]{:S(2)}) collective-permute-start(bf16[2,64,128]{2,1,0:T(8,128)(2,1)S(1)} %gather_fusion.7), channel_id=1, source_target_pairs={{2,0},{4,2},{6,4},{8,6},{10,8},{12,10},{14,12},{0,14},{3,1},{5,3},... | collective-permute-start | bytes 98312 | tf_op jit(solution)/shard_map/ppermute | solution.py:14
  116.5 2.0 collective-permute-start.6
  118.5 3.7 %collective-permute-done.6 = bf16[2,64,128]{2,1,0:T(8,128)(2,1)S(1)} collective-permute-done((bf16[2,64,128]{2,1,0:T(8,128)(2,1)S(1)}, bf16[2,64,128]{2,1,0:T(8,128)(2,1)S(1)}, u32[]{:S(2)}, u32[]{:S(2)}) %collective-permute-start.6) | collective-permute-done | bytes 32800 | tf_op jit(solution)/shard_map/ppermute | solution.py:14
  122.2 3.8 %collective-permute-start.7 = (bf16[2,64,128]{2,1,0:T(8,128)(2,1)S(1)}, bf16[2,64,128]{2,1,0:T(8,128)(2,1)S(1)}, u32[]{:S(2)}, u32[]{:S(2)}) collective-permute-start(bf16[2,64,128]{2,1,0:T(8,128)(2,1)S(1)} %gather_fusion.9), channel_id=1, source_target_pairs={{4,0},{6,2},{8,4},{10,6},{12,8},{14,10},{0,12},{2,14},{5,1},{7,3},... | collective-permute-start | bytes 98312 | tf_op jit(solution)/shard_map/ppermute | solution.py:14
  126.1 1.6 collective-permute-done.7
  152.7 1.8 collective-permute-start.8
  154.4 1.8 collective-permute-start.9
  156.2 3.8 %collective-permute-start.11 = (bf16[2,64,128]{2,1,0:T(8,128)(2,1)}, bf16[2,64,128]{2,1,0:T(8,128)(2,1)}, u32[]{:S(2)}, u32[]{:S(2)}) collective-permute-start(bf16[2,64,128]{2,1,0:T(8,128)(2,1)} %gather_fusion.15), channel_id=1, source_target_pairs={{4,0},{6,2},{8,4},{10,6},{12,8},{14,10},{0,12},{2,14},{5,1},{7,3},... | collective-permute-start | bytes 98312 | tf_op jit(solution)/shard_map/ppermute | solution.py:14
  161.1 1.9 pad_maximum_fusion.1
  163.8 3.3 %scatter_fusion.5 = f32[16,64,128]{2,1,0:T(8,128)} fusion(f32[16,64,128]{2,1,0:T(8,128)} %broadcast.94.clone.1, s32[16]{0:T(128)} %copy-done.71, f32[16,64,128]{2,1,0:T(8,128)} %pad_maximum_fusion.1), kind=kCustom, calls=%fused_computation.23 | custom fusion | flops 131072 | bytes 1572928 | tf_op jit(solution)/shard_map/scatter-add | solution.py:58
  167.2 1.8 fusion.89
  169.0 2.0 collective-permute-start.16
  171.1 1.6 convolution_add_fusion.1
  172.7 1.5 fusion.45
  174.2 1.6 fusion.46
  175.8 1.6 fusion.47
  182.5 3.8 %collective-permute-start.18 = (f32[2,64,128]{2,1,0:T(8,128)}, f32[2,64,128]{2,1,0:T(8,128)S(1)}, u32[]{:S(2)}, u32[]{:S(2)}) collective-permute-start(f32[2,64,128]{2,1,0:T(8,128)} %get-tuple-element.71), channel_id=1, source_target_pairs={{4,0},{6,2},{8,4},{10,6},{12,8},{14,10},{0,12},{2,14},{5,1},{7,3},... | collective-permute-start | bytes 196616 | tf_op jit(solution)/shard_map/ppermute | solution.py:14
  190.5 1.6 gather_fusion.16
  192.1 1.6 gather_fusion.17
  203.6 1.6 fusion.31
  210.5 2.2 scatter_fusion.10
  213.4 2.9 collective-permute-start.20
  216.3 3.8 %collective-permute-start.22 = (f32[2,64,128]{2,1,0:T(8,128)}, f32[2,64,128]{2,1,0:T(8,128)}, u32[]{:S(2)}, u32[]{:S(2)}) collective-permute-start(f32[2,64,128]{2,1,0:T(8,128)} %get-tuple-element.67), channel_id=1, source_target_pairs={{4,0},{6,2},{8,4},{10,6},{12,8},{14,10},{0,12},{2,14},{5,1},{7,3},... | collective-permute-start | bytes 196616 | tf_op jit(solution)/shard_map/ppermute | solution.py:14
  220.1 2.3 slice_add_fusion
  222.5 2.1 scatter_fusion.11
  224.5 2.1 scatter_fusion.12
  226.6 2.2 scatter_fusion.13
  228.8 2.1 scatter_fusion.14
  230.9 1.9 subtract_convert_fusion
  232.8 63.9 %all-reduce.5.cloned.1.call-done = f32[4,64,64]{2,1,0:T(8,128)} async-done(((f32[4,64,64]{2,1,0:T(8,128)}), f32[4,64,64]{2,1,0:T(8,128)}) %all-reduce.5.cloned.1.call-update) | async-done | bytes 65552 | tf_op jit(solution)/shard_map/psum | solution.py:124
  296.7 1.6 broadcast_multiply_fusion
  (344 shorter events, 107.7 us)
Async XLA Ops:
  7.2 17.1 %copy-start = (bf16[8,64,576]{2,1,0:T(8,128)(2,1)S(1)}, bf16[8,64,576]{2,1,0:T(8,128)(2,1)}, u32[]{:S(2)}) copy-start(bf16[8,64,576]{2,1,0:T(8,128)(2,1)} %param.11) | copy-start | bytes 1769476
  7.2 215.2 %all-reduce.3.cloned.1.call-start = ((), (), s32[]{:S(2)}) async-start(), calls=%async_computation | async-start | bytes 262144 | tf_op jit(solution)/shard_map/psum | solution.py:124
  11.9 77.9 %collective-permute-start = (bf16[2,64,128]{2,1,0:T(8,128)(2,1)}, bf16[2,64,128]{2,1,0:T(8,128)(2,1)}, u32[]{:S(2)}, u32[]{:S(2)}) collective-permute-start(bf16[2,64,128]{2,1,0:T(8,128)(2,1)} %gather_fusion), channel_id=1, source_target_pairs={{14,0},{0,2},{2,4},{4,6},{6,8},{8,10},{10,12},{12,14},{15,1},{1,3}... | collective-permute-start | bytes 98312 | tf_op jit(solution)/shard_map/ppermute | solution.py:14
  14.6 76.2 %collective-permute-start.1 = (bf16[2,64,128]{2,1,0:T(8,128)(2,1)}, bf16[2,64,128]{2,1,0:T(8,128)(2,1)}, u32[]{:S(2)}, u32[]{:S(2)}) collective-permute-start(bf16[2,64,128]{2,1,0:T(8,128)(2,1)} %gather_fusion.1), channel_id=1, source_target_pairs={{2,0},{4,2},{6,4},{8,6},{10,8},{12,10},{14,12},{0,14},{3,1},{5,3},... | collective-permute-start | bytes 98312 | tf_op jit(solution)/shard_map/ppermute | solution.py:14
  17.2 77.7 %collective-permute-start.2 = (bf16[2,64,128]{2,1,0:T(8,128)(2,1)}, bf16[2,64,128]{2,1,0:T(8,128)(2,1)}, u32[]{:S(2)}, u32[]{:S(2)}) collective-permute-start(bf16[2,64,128]{2,1,0:T(8,128)(2,1)} %gather_fusion.2), channel_id=1, source_target_pairs={{12,0},{14,2},{0,4},{2,6},{4,8},{6,10},{8,12},{10,14},{13,1},{15,3... | collective-permute-start | bytes 98312 | tf_op jit(solution)/shard_map/ppermute | solution.py:14
  20.0 75.8 %collective-permute-start.3 = (bf16[2,64,128]{2,1,0:T(8,128)(2,1)}, bf16[2,64,128]{2,1,0:T(8,128)(2,1)}, u32[]{:S(2)}, u32[]{:S(2)}) collective-permute-start(bf16[2,64,128]{2,1,0:T(8,128)(2,1)} %gather_fusion.3), channel_id=1, source_target_pairs={{4,0},{6,2},{8,4},{10,6},{12,8},{14,10},{0,12},{2,14},{5,1},{7,3},... | collective-permute-start | bytes 98312 | tf_op jit(solution)/shard_map/ppermute | solution.py:14
  31.6 109.3 %collective-permute-start.12 = (f32[2,64,128]{2,1,0:T(8,128)}, f32[2,64,128]{2,1,0:T(8,128)}, u32[]{:S(2)}, u32[]{:S(2)}) collective-permute-start(f32[2,64,128]{2,1,0:T(8,128)} %get-tuple-element.77), channel_id=1, source_target_pairs={{2,0},{4,2},{6,4},{8,6},{10,8},{12,10},{14,12},{0,14},{3,1},{5,3},... | collective-permute-start | bytes 196616 | tf_op jit(solution)/shard_map/ppermute | solution.py:14
  46.5 30.5 %copy-start.31 = (bf16[7,64,128]{2,1,0:T(8,128)(2,1)S(1)}, bf16[7,64,128]{2,1,0:T(8,128)(2,1)}, u32[]{:S(2)}) copy-start(bf16[7,64,128]{2,1,0:T(8,128)(2,1)} %get-tuple-element.110) | copy-start | bytes 344068
  46.5 33.4 %copy-start.36 = (bf16[6,64,128]{2,1,0:T(8,128)(2,1)S(1)}, bf16[6,64,128]{2,1,0:T(8,128)(2,1)}, u32[]{:S(2)}) copy-start(bf16[6,64,128]{2,1,0:T(8,128)(2,1)} %get-tuple-element.106) | copy-start | bytes 294916
  46.5 36.4 %copy-start.49 = (bf16[3,64,128]{2,1,0:T(8,128)(2,1)S(1)}, bf16[3,64,128]{2,1,0:T(8,128)(2,1)}, u32[]{:S(2)}) copy-start(bf16[3,64,128]{2,1,0:T(8,128)(2,1)} %get-tuple-element.104) | copy-start | bytes 147460
  48.9 35.5 %copy-start.34 = (f32[3,64,128]{2,1,0:T(8,128)S(1)}, f32[3,64,128]{2,1,0:T(8,128)}, u32[]{:S(2)}) copy-start(f32[3,64,128]{2,1,0:T(8,128)} %get-tuple-element.52) | copy-start | bytes 294916
  48.9 35.5 %copy-start.54 = (f32[1,64,128]{2,1,0:T(8,128)S(1)}, f32[1,64,128]{2,1,0:T(8,128)}, u32[]{:S(2)}) copy-start(f32[1,64,128]{2,1,0:T(8,128)} %get-tuple-element.60) | copy-start | bytes 98308
  89.8 52.5 %collective-permute-start.13 = (f32[2,64,128]{2,1,0:T(8,128)}, f32[2,64,128]{2,1,0:T(8,128)}, u32[]{:S(2)}, u32[]{:S(2)}) collective-permute-start(f32[2,64,128]{2,1,0:T(8,128)} %get-tuple-element.76), channel_id=1, source_target_pairs={{14,0},{0,2},{2,4},{4,6},{6,8},{8,10},{10,12},{12,14},{15,1},{1,3}... | collective-permute-start | bytes 196616 | tf_op jit(solution)/shard_map/ppermute | solution.py:14
  90.8 52.9 %collective-permute-start.14 = (f32[2,64,128]{2,1,0:T(8,128)}, f32[2,64,128]{2,1,0:T(8,128)}, u32[]{:S(2)}, u32[]{:S(2)}) collective-permute-start(f32[2,64,128]{2,1,0:T(8,128)} %get-tuple-element.75), channel_id=1, source_target_pairs={{4,0},{6,2},{8,4},{10,6},{12,8},{14,10},{0,12},{2,14},{5,1},{7,3},... | collective-permute-start | bytes 196616 | tf_op jit(solution)/shard_map/ppermute | solution.py:14
  94.9 50.3 %collective-permute-start.15 = (f32[2,64,128]{2,1,0:T(8,128)}, f32[2,64,128]{2,1,0:T(8,128)}, u32[]{:S(2)}, u32[]{:S(2)}) collective-permute-start(f32[2,64,128]{2,1,0:T(8,128)} %get-tuple-element.74), channel_id=1, source_target_pairs={{12,0},{14,2},{0,4},{2,6},{4,8},{6,10},{8,12},{10,14},{13,1},{15,3... | collective-permute-start | bytes 196616 | tf_op jit(solution)/shard_map/ppermute | solution.py:14
  104.3 6.7 %collective-permute-start.4 = (bf16[2,64,128]{2,1,0:T(8,128)(2,1)}, bf16[2,64,128]{2,1,0:T(8,128)(2,1)}, u32[]{:S(2)}, u32[]{:S(2)}) collective-permute-start(bf16[2,64,128]{2,1,0:T(8,128)(2,1)} %gather_fusion.6), channel_id=1, source_target_pairs={{14,0},{0,2},{2,4},{4,6},{6,8},{8,10},{10,12},{12,14},{15,1},{1,3}... | collective-permute-start | bytes 98312 | tf_op jit(solution)/shard_map/ppermute | solution.py:14
  111.0 5.5 %collective-permute-start.5 = (bf16[2,64,128]{2,1,0:T(8,128)(2,1)S(1)}, bf16[2,64,128]{2,1,0:T(8,128)(2,1)S(1)}, u32[]{:S(2)}, u32[]{:S(2)}) collective-permute-start(bf16[2,64,128]{2,1,0:T(8,128)(2,1)S(1)} %gather_fusion.7), channel_id=1, source_target_pairs={{2,0},{4,2},{6,4},{8,6},{10,8},{12,10},{14,12},{0,14},{3,1},{5,3},... | collective-permute-start | bytes 98312 | tf_op jit(solution)/shard_map/ppermute | solution.py:14
  116.5 5.7 %collective-permute-start.6 = (bf16[2,64,128]{2,1,0:T(8,128)(2,1)S(1)}, bf16[2,64,128]{2,1,0:T(8,128)(2,1)S(1)}, u32[]{:S(2)}, u32[]{:S(2)}) collective-permute-start(bf16[2,64,128]{2,1,0:T(8,128)(2,1)S(1)} %gather_fusion.8), channel_id=1, source_target_pairs={{12,0},{14,2},{0,4},{2,6},{4,8},{6,10},{8,12},{10,14},{13,1},{15,3... | collective-permute-start | bytes 98312 | tf_op jit(solution)/shard_map/ppermute | solution.py:14
  122.2 5.4 %collective-permute-start.7 = (bf16[2,64,128]{2,1,0:T(8,128)(2,1)S(1)}, bf16[2,64,128]{2,1,0:T(8,128)(2,1)S(1)}, u32[]{:S(2)}, u32[]{:S(2)}) collective-permute-start(bf16[2,64,128]{2,1,0:T(8,128)(2,1)S(1)} %gather_fusion.9), channel_id=1, source_target_pairs={{4,0},{6,2},{8,4},{10,6},{12,8},{14,10},{0,12},{2,14},{5,1},{7,3},... | collective-permute-start | bytes 98312 | tf_op jit(solution)/shard_map/ppermute | solution.py:14
  131.8 12.0 %copy-start.65 = (s32[2]{0:T(128)S(1)}, s32[2]{0:T(128)}, u32[]{:S(2)}) copy-start(s32[2]{0:T(128)} %copy-done.64) | copy-start | bytes 28
  131.8 13.4 %copy-start.61 = (s32[2]{0:T(128)S(1)}, s32[2]{0:T(128)}, u32[]{:S(2)}) copy-start(s32[2]{0:T(128)} %copy-done.60) | copy-start | bytes 28
  152.7 28.5 %collective-permute-start.8 = (bf16[2,64,128]{2,1,0:T(8,128)(2,1)}, bf16[2,64,128]{2,1,0:T(8,128)(2,1)}, u32[]{:S(2)}, u32[]{:S(2)}) collective-permute-start(bf16[2,64,128]{2,1,0:T(8,128)(2,1)} %gather_fusion.12), channel_id=1, source_target_pairs={{14,0},{0,2},{2,4},{4,6},{6,8},{8,10},{10,12},{12,14},{15,1},{1,3}... | collective-permute-start | bytes 98312 | tf_op jit(solution)/shard_map/ppermute | solution.py:14
  154.4 28.1 %collective-permute-start.9 = (bf16[2,64,128]{2,1,0:T(8,128)(2,1)}, bf16[2,64,128]{2,1,0:T(8,128)(2,1)}, u32[]{:S(2)}, u32[]{:S(2)}) collective-permute-start(bf16[2,64,128]{2,1,0:T(8,128)(2,1)} %gather_fusion.13), channel_id=1, source_target_pairs={{2,0},{4,2},{6,4},{8,6},{10,8},{12,10},{14,12},{0,14},{3,1},{5,3},... | collective-permute-start | bytes 98312 | tf_op jit(solution)/shard_map/ppermute | solution.py:14
  156.2 31.5 %collective-permute-start.10 = (bf16[2,64,128]{2,1,0:T(8,128)(2,1)}, bf16[2,64,128]{2,1,0:T(8,128)(2,1)}, u32[]{:S(2)}, u32[]{:S(2)}) collective-permute-start(bf16[2,64,128]{2,1,0:T(8,128)(2,1)} %gather_fusion.14), channel_id=1, source_target_pairs={{12,0},{14,2},{0,4},{2,6},{4,8},{6,10},{8,12},{10,14},{13,1},{15,3... | collective-permute-start | bytes 98312 | tf_op jit(solution)/shard_map/ppermute | solution.py:14
  156.2 32.9 %collective-permute-start.11 = (bf16[2,64,128]{2,1,0:T(8,128)(2,1)}, bf16[2,64,128]{2,1,0:T(8,128)(2,1)}, u32[]{:S(2)}, u32[]{:S(2)}) collective-permute-start(bf16[2,64,128]{2,1,0:T(8,128)(2,1)} %gather_fusion.15), channel_id=1, source_target_pairs={{4,0},{6,2},{8,4},{10,6},{12,8},{14,10},{0,12},{2,14},{5,1},{7,3},... | collective-permute-start | bytes 98312 | tf_op jit(solution)/shard_map/ppermute | solution.py:14
  167.1 11.7 %copy-start.48 = (bf16[3,64,128]{2,1,0:T(8,128)(2,1)S(1)}, bf16[3,64,128]{2,1,0:T(8,128)(2,1)}, u32[]{:S(2)}) copy-start(bf16[3,64,128]{2,1,0:T(8,128)(2,1)} %get-tuple-element.81) | copy-start | bytes 147460
  167.1 12.4 %copy-start.2 = (f32[16,64,128]{2,1,0:T(8,128)S(1)}, f32[16,64,128]{2,1,0:T(8,128)}, u32[]{:S(2)}) copy-start(f32[16,64,128]{2,1,0:T(8,128)} %scatter_fusion.5) | copy-start | bytes 1572868
  167.1 12.3 %copy-start.17 = (f32[7,64,128]{2,1,0:T(8,128)S(1)}, f32[7,64,128]{2,1,0:T(8,128)}, u32[]{:S(2)}) copy-start(f32[7,64,128]{2,1,0:T(8,128)} %get-tuple-element.48) | copy-start | bytes 688132
  167.1 12.3 %copy-start.18 = (f32[7,64,128]{2,1,0:T(8,128)S(1)}, f32[7,64,128]{2,1,0:T(8,128)}, u32[]{:S(2)}) copy-start(f32[7,64,128]{2,1,0:T(8,128)} %get-tuple-element.49) | copy-start | bytes 688132
  167.1 12.3 %copy-start.21 = (f32[6,64,128]{2,1,0:T(8,128)S(1)}, f32[6,64,128]{2,1,0:T(8,128)}, u32[]{:S(2)}) copy-start(f32[6,64,128]{2,1,0:T(8,128)} %get-tuple-element.44) | copy-start | bytes 589828
  167.1 12.3 %copy-start.22 = (f32[6,64,128]{2,1,0:T(8,128)S(1)}, f32[6,64,128]{2,1,0:T(8,128)}, u32[]{:S(2)}) copy-start(f32[6,64,128]{2,1,0:T(8,128)} %get-tuple-element.45) | copy-start | bytes 589828
  167.2 12.3 %copy-start.25 = (f32[5,64,128]{2,1,0:T(8,128)S(1)}, f32[5,64,128]{2,1,0:T(8,128)}, u32[]{:S(2)}) copy-start(f32[5,64,128]{2,1,0:T(8,128)} %get-tuple-element.40) | copy-start | bytes 491524
  167.2 12.3 %copy-start.26 = (f32[5,64,128]{2,1,0:T(8,128)S(1)}, f32[5,64,128]{2,1,0:T(8,128)}, u32[]{:S(2)}) copy-start(f32[5,64,128]{2,1,0:T(8,128)} %get-tuple-element.41) | copy-start | bytes 491524
  167.2 12.3 %copy-start.32 = (f32[3,64,128]{2,1,0:T(8,128)S(1)}, f32[3,64,128]{2,1,0:T(8,128)}, u32[]{:S(2)}) copy-start(f32[3,64,128]{2,1,0:T(8,128)} %get-tuple-element.38) | copy-start | bytes 294916
  167.2 12.3 %copy-start.33 = (f32[3,64,128]{2,1,0:T(8,128)S(1)}, f32[3,64,128]{2,1,0:T(8,128)}, u32[]{:S(2)}) copy-start(f32[3,64,128]{2,1,0:T(8,128)} %get-tuple-element.39) | copy-start | bytes 294916
  167.2 12.3 %copy-start.43 = (f32[2,64,128]{2,1,0:T(8,128)S(1)}, f32[2,64,128]{2,1,0:T(8,128)}, u32[]{:S(2)}) copy-start(f32[2,64,128]{2,1,0:T(8,128)} %get-tuple-element.42) | copy-start | bytes 196612
  167.2 12.3 %copy-start.44 = (f32[2,64,128]{2,1,0:T(8,128)S(1)}, f32[2,64,128]{2,1,0:T(8,128)}, u32[]{:S(2)}) copy-start(f32[2,64,128]{2,1,0:T(8,128)} %get-tuple-element.43) | copy-start | bytes 196612
  167.2 12.3 %copy-start.52 = (f32[1,64,128]{2,1,0:T(8,128)S(1)}, f32[1,64,128]{2,1,0:T(8,128)}, u32[]{:S(2)}) copy-start(f32[1,64,128]{2,1,0:T(8,128)} %get-tuple-element.46) | copy-start | bytes 98308
  167.2 12.3 %copy-start.53 = (f32[1,64,128]{2,1,0:T(8,128)S(1)}, f32[1,64,128]{2,1,0:T(8,128)}, u32[]{:S(2)}) copy-start(f32[1,64,128]{2,1,0:T(8,128)} %get-tuple-element.47) | copy-start | bytes 98308
  169.0 31.2 %collective-permute-start.16 = (f32[2,64,128]{2,1,0:T(8,128)}, f32[2,64,128]{2,1,0:T(8,128)}, u32[]{:S(2)}, u32[]{:S(2)}) collective-permute-start(f32[2,64,128]{2,1,0:T(8,128)} %get-tuple-element.73), channel_id=1, source_target_pairs={{2,0},{4,2},{6,4},{8,6},{10,8},{12,10},{14,12},{0,14},{3,1},{5,3},... | collective-permute-start | bytes 196616 | tf_op jit(solution)/shard_map/ppermute | solution.py:14
  181.1 20.5 %collective-permute-start.17 = (f32[2,64,128]{2,1,0:T(8,128)}, f32[2,64,128]{2,1,0:T(8,128)S(1)}, u32[]{:S(2)}, u32[]{:S(2)}) collective-permute-start(f32[2,64,128]{2,1,0:T(8,128)} %get-tuple-element.72), channel_id=1, source_target_pairs={{14,0},{0,2},{2,4},{4,6},{6,8},{8,10},{10,12},{12,14},{15,1},{1,3}... | collective-permute-start | bytes 196616 | tf_op jit(solution)/shard_map/ppermute | solution.py:14
  182.5 19.8 %collective-permute-start.18 = (f32[2,64,128]{2,1,0:T(8,128)}, f32[2,64,128]{2,1,0:T(8,128)S(1)}, u32[]{:S(2)}, u32[]{:S(2)}) collective-permute-start(f32[2,64,128]{2,1,0:T(8,128)} %get-tuple-element.71), channel_id=1, source_target_pairs={{4,0},{6,2},{8,4},{10,6},{12,8},{14,10},{0,12},{2,14},{5,1},{7,3},... | collective-permute-start | bytes 196616 | tf_op jit(solution)/shard_map/ppermute | solution.py:14
  187.7 15.2 %collective-permute-start.19 = (f32[2,64,128]{2,1,0:T(8,128)}, f32[2,64,128]{2,1,0:T(8,128)S(1)}, u32[]{:S(2)}, u32[]{:S(2)}) collective-permute-start(f32[2,64,128]{2,1,0:T(8,128)} %get-tuple-element.70), channel_id=1, source_target_pairs={{12,0},{14,2},{0,4},{2,6},{4,8},{6,10},{8,12},{10,14},{13,1},{15,3... | collective-permute-start | bytes 196616 | tf_op jit(solution)/shard_map/ppermute | solution.py:14
  198.1 98.6 %all-reduce.5.cloned.1.call-start = ((), (), s32[]{:S(2)}) async-start(), calls=%async_computation.1 | async-start | bytes 262144 | tf_op jit(solution)/shard_map/psum | solution.py:124
  213.4 9.1 %collective-permute-start.20 = (f32[2,64,128]{2,1,0:T(8,128)}, f32[2,64,128]{2,1,0:T(8,128)}, u32[]{:S(2)}, u32[]{:S(2)}) collective-permute-start(f32[2,64,128]{2,1,0:T(8,128)} %get-tuple-element.69), channel_id=1, source_target_pairs={{2,0},{4,2},{6,4},{8,6},{10,8},{12,10},{14,12},{0,14},{3,1},{5,3},... | collective-permute-start | bytes 196616 | tf_op jit(solution)/shard_map/ppermute | solution.py:14
  216.3 8.2 %collective-permute-start.21 = (f32[2,64,128]{2,1,0:T(8,128)}, f32[2,64,128]{2,1,0:T(8,128)}, u32[]{:S(2)}, u32[]{:S(2)}) collective-permute-start(f32[2,64,128]{2,1,0:T(8,128)} %get-tuple-element.68), channel_id=1, source_target_pairs={{14,0},{0,2},{2,4},{4,6},{6,8},{8,10},{10,12},{12,14},{15,1},{1,3}... | collective-permute-start | bytes 196616 | tf_op jit(solution)/shard_map/ppermute | solution.py:14
  216.3 10.3 %collective-permute-start.22 = (f32[2,64,128]{2,1,0:T(8,128)}, f32[2,64,128]{2,1,0:T(8,128)}, u32[]{:S(2)}, u32[]{:S(2)}) collective-permute-start(f32[2,64,128]{2,1,0:T(8,128)} %get-tuple-element.67), channel_id=1, source_target_pairs={{4,0},{6,2},{8,4},{10,6},{12,8},{14,10},{0,12},{2,14},{5,1},{7,3},... | collective-permute-start | bytes 196616 | tf_op jit(solution)/shard_map/ppermute | solution.py:14
  220.1 8.7 %collective-permute-start.23 = (f32[2,64,128]{2,1,0:T(8,128)}, f32[2,64,128]{2,1,0:T(8,128)}, u32[]{:S(2)}, u32[]{:S(2)}) collective-permute-start(f32[2,64,128]{2,1,0:T(8,128)} %get-tuple-element.66), channel_id=1, source_target_pairs={{12,0},{14,2},{0,4},{2,6},{4,8},{6,10},{8,12},{10,14},{13,1},{15,3... | collective-permute-start | bytes 196616 | tf_op jit(solution)/shard_map/ppermute | solution.py:14
  (54 other events, 267.6 us)
Sparse Core Ops, SparseCore 0:
  198.3 21.2 all-reduce.2
  222.9 73.7 all-reduce.4
